TPU v7x, 512 devices: a whole 4x4x16 slice. The times are simulated.
512 devices in a mesh: ctx: 64 (over z, y), head: 8 (over x, core).
Axes of the slice: x: 4, y: 4, z: 16, core: 2. Of those that a mesh axis runs over, the one named last changes fastest.
Arguments:
- query_lin: bfloat16 [8192, 256], P('ctx', 'head'), may hold values from -4 to 4
- key_lin: bfloat16 [8192, 256], P('ctx', 'head'), may hold values from -4 to 4
- values: bfloat16 [8192, 2048], P('ctx', 'head'), may hold values from -24 to 24
- win_queries: bfloat16 [8192, 2048], P('ctx', 'head'), may hold values from -6 to 6
- win_keys: bfloat16 [8192, 2048], P('ctx', 'head'), may hold values from -6 to 6
- gain: float32 [2048], P('head'), may hold values from 0.1 to 1.9
- grad_out: bfloat16 [8192, 2048], P('ctx', 'head'), may hold values from -6 to 6
Outputs:
- mixed_out: bfloat16 [8192, 2048], P('ctx', 'head')
- grad_query_lin: bfloat16 [8192, 256], P('ctx', 'head')
- grad_key_lin: bfloat16 [8192, 256], P('ctx', 'head')
- grad_values: bfloat16 [8192, 2048], P('ctx', 'head')
- grad_win_queries: bfloat16 [8192, 2048], P('ctx', 'head')
- grad_win_keys: bfloat16 [8192, 2048], P('ctx', 'head')
All inputs are finite; a program needn't handle non-finite values.
Results may differ from a plain program's by a relative error of at most 0.015.
Values may be sent and summed in bfloat16 or wider, within the bound.
A program may use at most 128 MiB of HBM per device.

v0:
```python
import math

import jax
import jax.numpy as jnp
from jax import lax
from jax.sharding import PartitionSpec as P

HEADS = 16
KD = 16
DV = 128
WD = 128
WINDOW = 128


epsilon = 1e-06


def from_behind(value, axis, by):
    size = lax.axis_size(axis)
    pairs = [(i, i + by) for i in range(size) if 0 <= i + by < size]
    return lax.ppermute(value, axis, pairs)


def prefix_2(value, axis, join, neutral, backward):
    count = lax.axis_size(axis)
    place = lax.axis_index(axis)
    ahead = count - 1 - place if backward else place
    gathered = lax.all_gather(value.astype(jnp.bfloat16), axis)
    state = jnp.zeros_like(value) + jnp.asarray(neutral, value.dtype)

    def one(step, state):
        source = count - 1 - step if backward else step
        return join(state, lax.dynamic_index_in_dim(gathered, source, 0, False).astype(value.dtype))

    return lax.fori_loop(0, ahead, one, state)


def features_cols(points):
    head_count = points.shape[0]
    key_depth = points.shape[1]
    tok_count = points.shape[2]
    linear_part = points / math.sqrt(math.sqrt(key_depth))
    outer_part = (points[:, :, None, :] * points[:, None, :, :]).reshape(
        head_count, key_depth * key_depth, tok_count
    )
    outer_part = outer_part / (math.sqrt(2.0) * math.sqrt(key_depth))
    return jnp.concatenate([jnp.ones_like(points[:, :1, :]), linear_part, outer_part], axis=1)


def accumulate(earlier, upcoming):
    return earlier + upcoming


def window_math(query_blocks, key_pairs, value_pairs, dout_blocks, allowed, scale_win):
    scores = (
        jnp.einsum("bthe,bshe->bhts", query_blocks, key_pairs, preferred_element_type=jnp.float32)
        * scale_win
    )
    row_top = jnp.max(jnp.where(allowed, scores, -jnp.inf), axis=-1, keepdims=True)
    weights = jnp.where(allowed, jnp.exp(scores - row_top), 0.0)
    row_total = jnp.sum(weights, axis=-1, keepdims=True)
    soft_probs = weights / row_total
    probs_round = soft_probs.astype(jnp.bfloat16)
    win_out = jnp.einsum(
        "bhts,bshd->bthd", probs_round, value_pairs, preferred_element_type=jnp.float32
    )
    grad_prob = jnp.einsum(
        "bthd,bshd->bhts", dout_blocks, value_pairs, preferred_element_type=jnp.float32
    )
    row_delta = jnp.transpose(
        jnp.sum(dout_blocks.astype(jnp.float32) * win_out, axis=-1), (0, 2, 1)
    )[..., None]
    grad_score = (soft_probs * (grad_prob - row_delta)).astype(jnp.bfloat16)
    grad_query = (
        jnp.einsum("bhts,bshe->bthe", grad_score, key_pairs, preferred_element_type=jnp.float32)
        * scale_win
    )
    grad_keys = (
        jnp.einsum("bhts,bthe->bshe", grad_score, query_blocks, preferred_element_type=jnp.float32)
        * scale_win
    )
    grad_vals = jnp.einsum(
        "bhts,bthd->bshd", probs_round, dout_blocks, preferred_element_type=jnp.float32
    )
    return (win_out, grad_query, grad_keys, grad_vals, row_top, row_total, row_delta)


def shards(query_lin, key_lin, values, win_queries, win_keys, gain, grad_out):
    tok_rows = query_lin.shape[0]
    head_count = values.shape[1] // DV
    full_width = HEADS * DV
    scale_lin = 1.0 / math.sqrt(KD)
    scale_win = 1.0 / math.sqrt(WD)
    ctx_index = lax.axis_index("ctx")
    tail_start = tok_rows - WINDOW
    rim_keys, rim_values = from_behind((win_keys, values), "ctx", 1)
    query_h = query_lin.reshape(tok_rows, head_count, KD)
    key_h = key_lin.reshape(tok_rows, head_count, KD)
    value_h = values.reshape(tok_rows, head_count, DV)
    query_cols = jnp.transpose(query_h, (1, 2, 0)).astype(jnp.float32)
    key_cols = jnp.transpose(key_h, (1, 2, 0)).astype(jnp.float32)
    query_feat, pull_query = jax.vjp(features_cols, query_cols)
    key_feat, pull_key = jax.vjp(features_cols, key_cols)
    query_phi = query_feat.astype(jnp.bfloat16)
    key_phi = key_feat.astype(jnp.bfloat16)
    local_state = jnp.einsum("hfs,shd->hfd", key_phi, value_h, preferred_element_type=jnp.float32)
    state_zero = jnp.zeros_like(local_state)
    prefix = prefix_2(local_state, "ctx", accumulate, state_zero, False)
    prefix_round = prefix.astype(jnp.bfloat16)
    lin_score = (
        jnp.einsum("thk,shk->hts", query_h, key_h, preferred_element_type=jnp.float32) * scale_lin
    )
    causal = jnp.tril(jnp.ones((tok_rows, tok_rows), jnp.bool_))
    kernel = jnp.where(causal, 1.0 + lin_score + 0.5 * lin_score * lin_score, 0.0).astype(
        jnp.bfloat16
    )
    linear_out = jnp.einsum("hts,shd->thd", kernel, value_h, preferred_element_type=jnp.float32)
    linear_out = linear_out + jnp.einsum(
        "hft,hfd->thd", query_phi, prefix_round, preferred_element_type=jnp.float32
    )
    linear_flat = linear_out.reshape(tok_rows, head_count * DV)
    dout_f = grad_out.astype(jnp.float32)
    square_sum = lax.psum(jnp.sum(linear_flat * linear_flat, axis=1), "head")
    inverse = (1.0 / jnp.sqrt(square_sum / full_width + epsilon))[:, None]
    blocks = tok_rows // WINDOW
    keys_ext = jnp.concatenate([rim_keys, win_keys], axis=0).reshape(
        blocks + 1, WINDOW, head_count, WD
    )
    values_ext = jnp.concatenate([rim_values, values], axis=0).reshape(
        blocks + 1, WINDOW, head_count, DV
    )
    key_pairs = jnp.concatenate([keys_ext[:-1], keys_ext[1:]], axis=1)
    value_pairs = jnp.concatenate([values_ext[:-1], values_ext[1:]], axis=1)
    query_blocks = win_queries.reshape(blocks, WINDOW, head_count, WD)
    dout_blocks = grad_out.reshape(blocks, WINDOW, head_count, DV)
    row_pos = jnp.arange(WINDOW, dtype=jnp.int32)[:, None]
    col_pos = jnp.arange(2 * WINDOW, dtype=jnp.int32)[None, :]
    band_mask = (col_pos > row_pos) & (col_pos <= row_pos + WINDOW)
    key_start = (
        ctx_index * tok_rows
        + jnp.arange(blocks, dtype=jnp.int32)[:, None, None] * WINDOW
        - WINDOW
        + col_pos[None]
    )
    allowed = (band_mask[None] & (key_start >= 0))[:, None]
    win_out, grad_wq, key_grads, value_grads, row_top, row_total, row_delta = window_math(
        query_blocks, key_pairs, value_pairs, dout_blocks, allowed, scale_win
    )
    window_flat = win_out.reshape(tok_rows, head_count * DV)
    mixed_out = (linear_flat * inverse * gain + window_flat).astype(jnp.bfloat16)
    cross_sum = lax.psum(jnp.sum(gain * dout_f * linear_flat, axis=1), "head")
    grad_lin = (
        inverse * gain * dout_f
        - linear_flat * inverse * inverse * inverse * (cross_sum / full_width)[:, None]
    ).astype(jnp.bfloat16)
    grad_lin_h = grad_lin.reshape(tok_rows, head_count, DV)
    value_dot = jnp.einsum("thd,shd->hts", grad_lin_h, value_h, preferred_element_type=jnp.float32)
    grad_score = jnp.where(causal, value_dot * (1.0 + lin_score), 0.0).astype(jnp.bfloat16)
    query_pull = jnp.einsum(
        "thd,hfd->hft", grad_lin_h, prefix_round, preferred_element_type=jnp.float32
    )
    grad_query = (
        jnp.einsum("hts,shk->thk", grad_score, key_h, preferred_element_type=jnp.float32)
        * scale_lin
    )
    grad_query = grad_query + jnp.transpose(pull_query(query_pull)[0], (2, 0, 1))
    local_back = jnp.einsum(
        "hft,thd->hfd", query_phi, grad_lin_h, preferred_element_type=jnp.float32
    )
    suffix = prefix_2(local_back, "ctx", accumulate, state_zero, True)
    suffix_round = suffix.astype(jnp.bfloat16)
    grad_value_lin = jnp.einsum(
        "hts,thd->shd", kernel, grad_lin_h, preferred_element_type=jnp.float32
    )
    grad_value_lin = grad_value_lin + jnp.einsum(
        "hfs,hfd->shd", key_phi, suffix_round, preferred_element_type=jnp.float32
    )
    key_pull = jnp.einsum("shd,hfd->hfs", value_h, suffix_round, preferred_element_type=jnp.float32)
    grad_key = (
        jnp.einsum("hts,thk->shk", grad_score, query_h, preferred_element_type=jnp.float32)
        * scale_lin
    )
    grad_key = grad_key + jnp.transpose(pull_key(key_pull)[0], (2, 0, 1))
    pad_tail = ((0, 1), (0, 0), (0, 0), (0, 0))
    pad_head = ((1, 0), (0, 0), (0, 0), (0, 0))
    key_ext_grad = jnp.pad(key_grads[:, :WINDOW], pad_tail) + jnp.pad(
        key_grads[:, WINDOW:], pad_head
    )
    value_ext_grad = jnp.pad(value_grads[:, :WINDOW], pad_tail) + jnp.pad(
        value_grads[:, WINDOW:], pad_head
    )
    key_own = key_ext_grad[1:].reshape(tok_rows, head_count * WD)
    value_own = value_ext_grad[1:].reshape(tok_rows, head_count * DV)
    back_keys, back_values = (
        from_behind(
            key_ext_grad[0].reshape(WINDOW, head_count * WD).astype(jnp.bfloat16), "ctx", -1
        ).astype(jnp.float32),
        from_behind(
            value_ext_grad[0].reshape(WINDOW, head_count * DV).astype(jnp.bfloat16), "ctx", -1
        ).astype(jnp.float32),
    )
    key_own = jnp.concatenate([key_own[:tail_start], key_own + back_keys], axis=0)
    value_own = jnp.concatenate([value_own[:tail_start], value_own + back_values], axis=0)
    grad_query_lin = grad_query.astype(jnp.bfloat16).reshape(tok_rows, head_count * KD)
    grad_key_lin = grad_key.astype(jnp.bfloat16).reshape(tok_rows, head_count * KD)
    grad_values = (grad_value_lin.reshape(tok_rows, head_count * DV) + value_own).astype(
        jnp.bfloat16
    )
    grad_win_queries = grad_wq.reshape(tok_rows, head_count * WD).astype(jnp.bfloat16)
    grad_win_keys = key_own.astype(jnp.bfloat16)
    return (mixed_out, grad_query_lin, grad_key_lin, grad_values, grad_win_queries, grad_win_keys)


def solution(mesh):
    placed = (
        P("ctx", "head"),
        P("ctx", "head"),
        P("ctx", "head"),
        P("ctx", "head"),
        P("ctx", "head"),
        P("head"),
        P("ctx", "head"),
    )
    return jax.shard_map(
        shards,
        mesh=mesh,
        in_specs=placed,
        out_specs=(
            P("ctx", "head"),
            P("ctx", "head"),
            P("ctx", "head"),
            P("ctx", "head"),
            P("ctx", "head"),
            P("ctx", "head"),
        ),
        check_vma=False,
    )
```

profile of v0, /device:TPU:24, one launch (start us, length us, event | category | flops | bytes accessed | tf_op | source)
XLA Modules:
  0.0 465.6 jit_solution(8082545731358047730)
XLA Ops:
  8.7 1.8 convolution_convert_fusion.1
  10.6 3.5 collective-permute-start
  15.0 3.5 collective-permute-start.1
  19.6 1.0 copy.121
  25.0 147.9 %all-gather.5.cloned.1.call-done = bf16[128,273,128]{2,1,0:T(8,128)(2,1)} async-done(((bf16[2,273,128]{2,1,0:T(8,128)(2,1)}), bf16[128,273,128]{2,1,0:T(8,128)(2,1)}) %all-gather.5.cloned.1.call-update) | async-done | bytes 8945680 | tf_op jit(solution)/shard_map/all_gather | solution.py:28
  173.0 2.9 while.22
  176.7 12.4 %all-reduce.4 = (f32[128]{0:T(128)S(1)}, f32[128]{0:T(128)S(1)}) all-reduce(f32[128]{0:T(128)S(1)} %get-tuple-element.137, f32[128]{0:T(128)S(1)} %multiply_reduce_fusion.4), channel_id=1, replica_groups=mesh['ctx'=64,'head'=8] {'head'}, use_global_device_ids=true, to_apply=%region_3.4 | all-reduce | flops 256 | bytes 2048 | tf_op jit(solution)/shard_map/psum | solution.py:123
  190.0 1.0 convolution_convert_fusion
  192.6 2.4 collective-permute-start.3
  195.6 1.9 collective-permute-start.2
  197.6 3.5 collective-permute-done.3
  203.2 194.5 %all-gather.7.cloned.1.call-done = bf16[128,273,128]{2,1,0:T(8,128)(2,1)} async-done(((bf16[2,273,128]{2,1,0:T(8,128)(2,1)}), bf16[128,273,128]{2,1,0:T(8,128)(2,1)}) %all-gather.7.cloned.1.call-update) | async-done | bytes 8945680 | tf_op jit(solution)/shard_map/all_gather | solution.py:28
  397.7 58.6 %while.23 = (s32[]{:T(128)}, f32[2,273,128]{2,1,0:T(8,128)S(1)}, s32[]{:T(128)}, bf16[64,2,273,128]{3,2,1,0:T(8,128)(2,1)}, s32[]{:T(128)}, /*index=5*/s32[]{:T(128)}, s32[]{:T(128)}, s32[]{:T(128)}) while((s32[]{:T(128)}, f32[2,273,128]{2,1,0:T(8,128)S(1)}, s32[]{:T(128)}, bf16[64,2,273,128]{3,2,1,0:T(8,128)(2,1)}, s32[]{:T(128)}, ...), condition=%wide.region_11.12_spmd, body=%wide.region_10.11_spmd.sunk | while | flops 139782 | bytes 699023 | solution.py:35
  399.7 1.0 convert_add_fusion.5
  400.7 1.0 convert_add_fusion.5
  401.6 1.0 convert_add_fusion.5
  402.6 1.0 convert_add_fusion.5
  403.6 1.0 convert_add_fusion.5
  409.5 1.0 convert_add_fusion.5
  410.4 1.0 convert_add_fusion.5
  411.4 1.0 convert_add_fusion.5
  412.4 1.0 convert_add_fusion.5
  413.4 1.0 convert_add_fusion.5
  418.3 1.0 convert_add_fusion.5
  (128 shorter events, 65.9 us)
Async XLA Ops:
  7.2 169.1 %copy-start = (bf16[128,256]{1,0:T(8,128)(2,1)S(1)}, bf16[128,256]{1,0:T(8,128)(2,1)}, u32[]{:S(2)}) copy-start(bf16[128,256]{1,0:T(8,128)(2,1)} %param.13) | copy-start | bytes 196612
  7.2 169.4 %copy-start.1 = (bf16[128,256]{1,0:T(8,128)(2,1)S(1)}, bf16[128,256]{1,0:T(8,128)(2,1)}, u32[]{:S(2)}) copy-start(bf16[128,256]{1,0:T(8,128)(2,1)} %param.17) | copy-start | bytes 196612
  7.2 169.4 %copy-start.4 = (f32[256]{0:T(256)S(1)}, f32[256]{0:T(256)}, u32[]{:S(2)}) copy-start(f32[256]{0:T(256)} %param.16) | copy-start | bytes 3076
  7.2 165.7 %all-gather.5.cloned.1.call-start = ((), (), s32[]{:S(2)}) async-start(), calls=%async_computation | async-start | bytes 9318400 | tf_op jit(solution)/shard_map/all_gather | solution.py:28
  10.5 387.2 %all-gather.7.cloned.1.call-start = ((), (), s32[]{:S(2)}) async-start(), calls=%async_computation.1 | async-start | bytes 9318400 | tf_op jit(solution)/shard_map/all_gather | solution.py:28
  10.6 13.6 %collective-permute-start = (bf16[128,256]{1,0:T(8,128)(2,1)}, bf16[128,256]{1,0:T(8,128)(2,1)S(1)}, u32[]{:S(2)}, u32[]{:S(2)}) collective-permute-start(bf16[128,256]{1,0:T(8,128)(2,1)} %param.13), channel_id=1, source_target_pairs={{0,8},{8,16},{16,24},{24,32},{32,40},{40,48},{48,56},{56,64},{64,7... | collective-permute-start | bytes 196616 | tf_op jit(solution)/shard_map/ppermute | solution.py:21
  15.0 9.0 %collective-permute-start.1 = (bf16[128,256]{0,1:T(8,128)(2,1)S(1)}, bf16[128,256]{0,1:T(8,128)(2,1)S(1)}, u32[]{:S(2)}, u32[]{:S(2)}) collective-permute-start(bf16[128,256]{0,1:T(8,128)(2,1)S(1)} %copy.83), channel_id=1, source_target_pairs={{0,8},{8,16},{16,24},{24,32},{32,40},{40,48},{48,56},{56,64},{64,7... | collective-permute-start | bytes 196616 | tf_op jit(solution)/shard_map/ppermute | solution.py:21
  24.3 178.1 %copy-start.2 = (bf16[128,32]{0,1:T(8,128)(2,1)S(1)}, bf16[128,32]{0,1:T(8,128)(2,1)}, u32[]{:S(2)}) copy-start(bf16[128,32]{0,1:T(8,128)(2,1)} %param.12) | copy-start | bytes 24580
  175.9 281.3 %copy-start.3 = (bf16[128,32]{0,1:T(8,128)(2,1)S(1)}, bf16[128,32]{0,1:T(8,128)(2,1)}, u32[]{:S(2)}) copy-start(bf16[128,32]{0,1:T(8,128)(2,1)} %param.11) | copy-start | bytes 24580
  192.6 8.4 %collective-permute-start.3 = (bf16[128,256]{0,1:T(8,128)(2,1)S(1)}, bf16[128,256]{0,1:T(8,128)(2,1)S(1)}, u32[]{:S(2)}, u32[]{:S(2)}) collective-permute-start(bf16[128,256]{0,1:T(8,128)(2,1)S(1)} %bitcast.205), channel_id=1, source_target_pairs={{8,0},{16,8},{24,16},{32,24},{40,32},{48,40},{56,48},{64,56},{72,6... | collective-permute-start | bytes 196616 | tf_op jit(solution)/shard_map/ppermute | solution.py:21
  195.6 262.5 %collective-permute-start.2 = (bf16[128,256]{1,0:T(8,128)(2,1)S(1)}, bf16[128,256]{1,0:T(8,128)(2,1)S(1)}, u32[]{:S(2)}, u32[]{:S(2)}) collective-permute-start(bf16[128,256]{1,0:T(8,128)(2,1)S(1)} %copy.99), channel_id=1, source_target_pairs={{8,0},{16,8},{24,16},{32,24},{40,32},{48,40},{56,48},{64,56},{72,6... | collective-permute-start | bytes 196616 | tf_op jit(solution)/shard_map/ppermute | solution.py:21
Sparse Core Ops, SparseCore 0:
  11.0 161.8 all-gather.4
  191.1 206.5 all-gather.6
where the time goes:
time: 473 us; the launch traced here: 466 us
  waiting for transfers between devices  346 us (73%)
  other arithmetic  65.1 us (14%)
  between operations  14.5 us (3%)
  blocking collectives  12.4 us (3%)
  starting transfers between devices  11.4 us (2%)
  matrix products  8.26 us (2%)
  local copies, waits for them, and re-layouts  6.56 us (1%)
    all_gather x2, waiting for transfers between devices, prefix_2(): gathered = lax.all_gather(value.astype(jnp.bfloat16), axis)  342 us
    add x63, other arithmetic, accumulate(): return earlier + upcoming  60.1 us
    psum x1, blocking collectives, shards(): square_sum = lax.psum(jnp.sum(linear_flat * linear_flat, axis=1), 'head')  12.4 us
    ppermute x4, starting transfers between devices, from_behind(): return lax.ppermute(value, axis, pairs)  11.3 us
  transfers between devices with their start and end apart: 6, of which 3 were waited for; matrix products, arithmetic and copies ran while one was open for 15% of the time, Pallas kernels for 0%

commit v1 on v0

v1 whole, which is shorter than its diff:
```python
import math

import jax
import jax.numpy as jnp
import numpy as np
from jax import lax
from jax.experimental import pallas as pl
from jax.experimental.pallas import tpu as pltpu
from jax.sharding import PartitionSpec as P

HEADS = 16
KD = 16
DV = 128
WD = 128
TOK = 128
NY = 4
NZ = 16
NH = 8
ROWS = 160
HALF = ROWS // 2
WIDTH = HEADS * DV
EPS = 1e-06
MESH = pl.DeviceIdType.MESH
BF = jnp.bfloat16
F32 = jnp.float32


def selectors():
    first = np.zeros((2 * ROWS, 2 * KD), np.float32)
    second = np.zeros((2 * ROWS, 2 * KD), np.float32)
    for h in range(2):
        base, lane = h * ROWS, h * KD
        for i in range(KD):
            first[base + 1 + i, lane + i] = 1
            first[base + 17 + i, lane + i] = 1
            second[base + 17 + i, lane + i] = 1
        row = base + 33
        for i in range(KD):
            for j in range(i + 1, KD):
                first[row, lane + i] = 1
                second[row, lane + j] = 1
                row += 1
    return first, second


def nn(a, b):
    return lax.dot_general(a, b, (((1,), (0,)), ((), ())), preferred_element_type=F32)


def nt(a, b):
    return lax.dot_general(a, b, (((1,), (1,)), ((), ())), preferred_element_type=F32)


def tn(a, b):
    return lax.dot_general(a, b, (((0,), (0,)), ((), ())), preferred_element_type=F32)


def kernel(
    ql_ref, kl_ref, v_ref, wq_ref, wk_ref, gain_ref, do_ref, e1_ref, e2_ref,
    mixed_ref, gql_ref, gkl_ref, gv_ref, gwq_ref, gwk_ref,
    krim, vrim, gkout, gvout, gkin, gvin,
    st_a, r1_a, t_a, rz_a, w_a, rw_a, out_a, pre_a,
    st_b, r1_b, t_b, rz_b, w_b, rw_b, out_b, pre_b,
    sums, sums_in, lin_sc, win_sc, ker_sc, gvacc, gkacc, phiq_sc, phik_sc,
    ss, rs,
):
    ctx = lax.axis_index("ctx")
    head = lax.axis_index("head")
    z = ctx // NY
    y = lax.rem(ctx, NY)
    sends = []

    def at(zz, yy):
        return {"ctx": lax.rem(zz + NZ, NZ) * NY + lax.rem(yy + NY, NY)}

    ahead = {"ctx": lax.rem(ctx + 1, NZ * NY)}
    behind = {"ctx": lax.rem(ctx + NZ * NY - 1, NZ * NY)}

    barrier = pltpu.get_barrier_semaphore()
    peers = [at(z, y + d) for d in (1, 2, 3)]
    peers += [at(z + d, y) for d in (1, 2, 3, 4, 8, -4, -3, -2, -1)]
    peers += [ahead, behind]
    peers += [{"head": lax.rem(head + d, NH)} for d in range(1, NH)]
    for peer in peers:
        pl.semaphore_signal(barrier, inc=1, device_id=peer, device_id_type=MESH)

    def send(src, dst, slot, device):
        copy = pltpu.make_async_remote_copy(
            src_ref=src, dst_ref=dst, send_sem=ss.at[slot], recv_sem=rs.at[slot],
            device_id=device, device_id_type=MESH,
        )
        copy.start()
        sends.append(copy)
        return copy

    def wait_all(copies):
        for copy in copies:
            copy.wait_recv()

    def flag(cond):
        return jnp.where(cond, 1.0, 0.0).astype(F32)

    class Scan:
        def __init__(self, sign, base, st, r1, t, rz, w, rw, out, pre):
            self.sign, self.base = sign, base
            self.st, self.r1, self.t, self.rz = st, r1, t, rz
            self.w, self.rw, self.out, self.pre = w, rw, out, pre

        def start(self):
            self.c1 = [
                send(self.st.at[lax.rem(y + d, NY)], self.r1.at[d - 1], self.base + d - 1, at(z, y + d))
                for d in (1, 2, 3)
            ]

        def parts(self):
            return [self.st[y].astype(F32)] + [self.r1[d].astype(F32) for d in range(3)]

        def rows(self):
            wait_all(self.c1)
            p = self.parts()
            self.t[...] = ((p[0] + p[1]) + (p[2] + p[3])).astype(BF)
            self.c2 = [
                send(self.t, self.rz.at[j - 1], self.base + 2 + j, at(z + self.sign * j, y))
                for j in (1, 2, 3)
            ]

        def holds(self, j):
            return flag(z - j >= 0) if self.sign > 0 else flag(z + j < NZ)

        def near(self):
            total = self.rz[0].astype(F32) * self.holds(1)
            for j in (2, 3):
                total = total + self.rz[j - 1].astype(F32) * self.holds(j)
            return total

        def windows(self):
            wait_all(self.c2)
            p = self.parts()
            self.w[...] = ((p[0] + p[1]) + (p[2] + p[3]) + self.near()).astype(BF)
            self.c3 = [
                send(self.w, self.rw.at[j - 1], self.base + 5 + j, at(z + self.sign * 4 * j, y))
                for j in (2, 1, 3)
            ]

        def spread(self):
            wait_all(self.c3)
            total = self.near()
            for j in (1, 2, 3):
                total = total + self.rw[j - 1].astype(F32) * self.holds(4 * j)
            p = self.parts()
            self.c4 = []
            for e in (2, 1, 3, 0):
                dest = lax.rem(y + e, NY)
                mine = total
                for d in range(NY):
                    source = lax.rem(y + NY - d, NY)
                    earlier = source < dest if self.sign > 0 else source > dest
                    mine = mine + p[d] * flag(earlier)
                if e == 0:
                    self.pre[y] = mine.astype(BF)
                else:
                    self.out[e - 1] = mine.astype(BF)
                    self.c4.append(
                        send(self.out.at[e - 1], self.pre.at[y], self.base + 8 + e, at(z, y + e))
                    )

        def finish(self):
            wait_all(self.c4)

    fwd = Scan(1, 0, st_a, r1_a, t_a, rz_a, w_a, rw_a, out_a, pre_a)
    bwd = Scan(-1, 12, st_b, r1_b, t_b, rz_b, w_b, rw_b, out_b, pre_b)

    lane32 = lax.broadcasted_iota(jnp.int32, (TOK, 2 * KD), 1)
    row = lax.broadcasted_iota(jnp.int32, (TOK, TOK), 0)
    col = lax.broadcasted_iota(jnp.int32, (TOK, TOK), 1)
    causal = col <= row
    frow = lax.broadcasted_iota(jnp.int32, (ROWS, TOK), 0)
    add_first = jnp.where(frow == 0, 1.0, 0.0)
    add_second = jnp.where(frow <= KD, 1.0, 0.0)
    pair_scale = 1.0 / (math.sqrt(2.0) * math.sqrt(KD))
    scale = jnp.where(frow == 0, 1.0, jnp.where(frow <= KD, 1.0 / math.sqrt(math.sqrt(KD)), pair_scale))
    weight = jnp.where(frow >= 33, 2.0, 1.0)

    def factors(x, h):
        rows = slice(h * ROWS, (h + 1) * ROWS)
        return nt(e1_ref[rows, :], x) + add_first, nt(e2_ref[rows, :], x) + add_second

    def phi(x, h):
        a, b = factors(x, h)
        return (a * b * scale).astype(BF)

    def heavy(features):
        return (features.astype(F32) * weight).astype(BF)

    def pull(x, h, cot):
        a, b = factors(x, h)
        rows = slice(h * ROWS, (h + 1) * ROWS)
        cot = cot * (scale * weight)
        return tn((cot * b).astype(BF), e1_ref[rows, :]) + tn((cot * a).astype(BF), e2_ref[rows, :])

    def own(x, h):
        inside = (lane32 >= h * KD) & (lane32 < (h + 1) * KD)
        return jnp.where(inside, x.astype(F32), 0.0).astype(BF)

    cols = [slice(h * DV, (h + 1) * DV) for h in range(2)]
    ql, kl = ql_ref[...], kl_ref[...]

    for h in range(2):
        key_phi = phi(kl, h)
        phik_sc[h] = key_phi
        state = nn(key_phi, v_ref[:, cols[h]])
        st_a[2 * h] = state[:HALF].astype(BF)
        st_a[2 * h + 1] = state[HALF:].astype(BF)

    pl.semaphore_wait(barrier, len(peers))
    fwd.start()
    rim = [
        send(wk_ref, krim, 24, ahead),
        send(v_ref, vrim, 25, ahead),
    ]

    def lin_score(h):
        return nt(own(ql, h), kl) * (1.0 / math.sqrt(KD))

    for h in range(2):
        phiq_sc[h] = phi(ql, h)
        s = lin_score(h)
        ker = jnp.where(causal, 1.0 + s + 0.5 * s * s, 0.0).astype(BF)
        ker_sc[h] = ker
        lin_sc[:, cols[h]] = nn(ker, v_ref[:, cols[h]])

    fwd.rows()

    scale_win = 1.0 / math.sqrt(WD)
    edge = (col > row) & (ctx > 0)
    wait_all(rim)

    def window(h):
        c = cols[h]
        q, k1, k2 = wq_ref[:, c], krim[:, c], wk_ref[:, c]
        v1, v2, do = vrim[:, c], v_ref[:, c], do_ref[:, c]
        s1 = jnp.where(edge, nt(q, k1) * scale_win, -1e30)
        s2 = jnp.where(causal, nt(q, k2) * scale_win, -1e30)
        top = jnp.maximum(
            jnp.max(s1, axis=1, keepdims=True), jnp.max(s2, axis=1, keepdims=True)
        )
        x1 = jnp.where(edge, jnp.exp(s1 - top), 0.0)
        x2 = jnp.where(causal, jnp.exp(s2 - top), 0.0)
        inv = 1.0 / (jnp.sum(x1, axis=1, keepdims=True) + jnp.sum(x2, axis=1, keepdims=True))
        p1, p2 = x1 * inv, x2 * inv
        b1, b2 = p1.astype(BF), p2.astype(BF)
        out = nn(b1, v1) + nn(b2, v2)
        win_sc[:, c] = out
        delta = jnp.sum(do.astype(F32) * out, axis=1, keepdims=True)
        g1 = (p1 * (nt(do, v1) - delta)).astype(BF)
        g2 = (p2 * (nt(do, v2) - delta)).astype(BF)
        gkout[:, c] = (tn(g1, q) * scale_win).astype(BF)
        gvout[:, c] = tn(b1, do).astype(BF)
        gwq_ref[:, c] = ((nn(g1, k1) + nn(g2, k2)) * scale_win).astype(BF)
        gkacc[:, c] = tn(g2, q) * scale_win
        gvacc[:, c] = tn(b2, do)

    window(0)
    fwd.windows()
    window(1)
    fwd.spread()
    back = [
        send(gkout, gkin, 26, behind),
        send(gvout, gvin, 27, behind),
    ]
    fwd.finish()

    gain = gain_ref[...]
    for h in range(2):
        prefix = pre_a[2 * h : 2 * h + 2].reshape(ROWS, DV)
        lin_sc[:, cols[h]] += tn(heavy(phiq_sc[h]), prefix)
    lin = lin_sc[...]
    gd = gain * do_ref[...].astype(F32)
    square = jnp.sum(lin * lin, axis=1, keepdims=True)
    cross = jnp.sum(gd * lin, axis=1, keepdims=True)
    both = jnp.where(col == 0, square, jnp.where(col == 1, cross, 0.0))
    sums[...] = both.T[:8]
    shares = [
        send(sums, sums_in.at[d - 1], 27 + d, {"head": lax.rem(head + d, NH)})
        for d in range(1, NH)
    ]
    wait_all(shares)
    total = sums[...]
    for d in range(NH - 1):
        total = total + sums_in[d]
    total = jnp.concatenate([total, jnp.zeros((TOK - 8, TOK), F32)], axis=0).T
    square = jnp.sum(jnp.where(col == 0, total, 0.0), axis=1, keepdims=True)
    cross = jnp.sum(jnp.where(col == 1, total, 0.0), axis=1, keepdims=True)
    inverse = 1.0 / jnp.sqrt(square * (1.0 / WIDTH) + EPS)
    grad_lin = (
        inverse * gd - lin * (inverse * inverse * inverse * (cross * (1.0 / WIDTH)))
    ).astype(BF)
    for h in range(2):
        state = nn(phiq_sc[h], grad_lin[:, cols[h]])
        st_b[2 * h] = state[:HALF].astype(BF)
        st_b[2 * h + 1] = state[HALF:].astype(BF)
    bwd.start()
    mixed_ref[...] = (lin * inverse * gain + win_sc[...]).astype(BF)

    gq = jnp.zeros((TOK, 2 * KD), F32)
    gk = jnp.zeros((TOK, 2 * KD), F32)
    for h in range(2):
        gl = grad_lin[:, cols[h]]
        g = nt(gl, v_ref[:, cols[h]]) * (1.0 + lin_score(h))
        g = jnp.where(causal, g, 0.0).astype(BF)
        gq = gq + nn(g, own(kl, h)) * (1.0 / math.sqrt(KD))
        gk = gk + tn(g, own(ql, h)) * (1.0 / math.sqrt(KD))
        if h == 0:
            bwd.rows()
    for h in range(2):
        gl = grad_lin[:, cols[h]]
        prefix = pre_a[2 * h : 2 * h + 2].reshape(ROWS, DV)
        gq = gq + pull(ql, h, nt(prefix, gl))
        gvacc[:, cols[h]] += tn(ker_sc[h], gl)
    gql_ref[...] = gq.astype(BF)
    bwd.windows()
    wait_all(back)
    gwk_ref[...] = (gkacc[...] + gkin[...].astype(F32)).astype(BF)
    gvacc[...] += gvin[...].astype(F32)
    bwd.spread()
    bwd.finish()
    for h in range(2):
        suffix = pre_b[2 * h : 2 * h + 2].reshape(ROWS, DV)
        gv_ref[:, cols[h]] = (gvacc[:, cols[h]] + tn(heavy(phik_sc[h]), suffix)).astype(BF)
        gk = gk + pull(kl, h, nt(suffix, v_ref[:, cols[h]]))
    gkl_ref[...] = gk.astype(BF)
    for copy in sends:
        copy.wait_send()


def shards(query_lin, key_lin, values, win_queries, win_keys, gain, grad_out):
    first, second = selectors()
    wide = jax.ShapeDtypeStruct((TOK, 2 * DV), BF)
    thin = jax.ShapeDtypeStruct((TOK, 2 * KD), BF)
    spec = pl.BlockSpec(memory_space=pltpu.VMEM)
    full = pltpu.VMEM((TOK, 2 * DV), BF)
    full32 = pltpu.VMEM((TOK, 2 * DV), F32)
    one = pltpu.VMEM((HALF, DV), BF)
    three = pltpu.VMEM((3, HALF, DV), BF)
    four = pltpu.VMEM((4, HALF, DV), BF)
    scan = [four, three, one, three, one, three, three, four]
    return pl.pallas_call(
        kernel,
        out_shape=(wide, thin, thin, wide, wide, wide),
        in_specs=[spec] * 9,
        out_specs=(spec,) * 6,
        scratch_shapes=[full] * 6
        + scan
        + scan
        + [
            pltpu.VMEM((8, TOK), F32),
            pltpu.VMEM((NH - 1, 8, TOK), F32),
            full32,
            full32,
            pltpu.VMEM((2, TOK, TOK), BF),
            full32,
            full32,
            pltpu.VMEM((2, ROWS, TOK), BF),
            pltpu.VMEM((2, ROWS, TOK), BF),
            pltpu.SemaphoreType.DMA((35,)),
            pltpu.SemaphoreType.DMA((35,)),
        ],
        compiler_params=pltpu.CompilerParams(collective_id=0, has_side_effects=True),
    )(
        query_lin, key_lin, values, win_queries, win_keys, gain.reshape(1, -1), grad_out,
        jnp.asarray(first, BF), jnp.asarray(second, BF),
    )


def solution(mesh):
    tiled = P("ctx", "head")
    return jax.shard_map(
        shards,
        mesh=mesh,
        in_specs=(tiled, tiled, tiled, tiled, tiled, P("head"), tiled),
        out_specs=(tiled,) * 6,
        check_vma=False,
    )
```

time: 473 us -> 75.9 us (0.16)
  the two profiles are of different devices: /device:TPU:24 before, /device:TPU:64 now
where the time goes in v1:
time: 75.9 us; the launch traced here: 75.4 us
  Pallas kernels  66.5 us (88%)
  local copies, waits for them, and re-layouts  8.26 us (11%)
    pallas_call x1, Pallas kernels, shards(): pl.pallas_call(kernel, out_shape=(wide, thin, thin, wide, wide, wide), in...  66.5 us
    unnamed x16, local copies, waits for them, and re-layouts  5.36 us
    pallas_call x2, local copies, waits for them, and re-layouts, shards(): pl.pallas_call(kernel, out_shape=(wide, thin, thin, wide, wide, wide), in...  2.9 us

profile of v1, /device:TPU:64, one launch (start us, length us, event | category | flops | bytes accessed | tf_op | source)
XLA Modules:
  0.0 75.4 jit_solution(17899391831211115741)
XLA Ops:
  0.6 0.0 copy-start.4
  0.6 1.4 %copy.15.ql_ref = bf16[128,32]{1,0:T(8,128)(2,1)} copy(bf16[128,32]{0,1:T(8,128)(2,1)} %param.9) | data formatting | bytes 16384 | tf_op args[0]
  2.1 0.0 copy-done.4
  2.1 0.7 copy.16.kl_ref
  2.8 66.5 %shard_map.136 = (bf16[128,256]{1,0:T(8,128)(2,1)}, bf16[128,32]{1,0:T(8,128)(2,1)}, bf16[128,32]{1,0:T(8,128)(2,1)}, bf16[128,256]{1,0:T(8,128)(2,1)}, bf16[128...) custom-call(bf16[128,32]{1,0:T(8,128)(2,1)} %copy.15.ql_ref, bf16[128,32]{1,0:T(8,128)(2,1)} %copy.16.kl_ref, ...), custom_call_target="tpu_custom_call" | custom-call | tf_op jit(solution)/shard_map/pallas_call | solution.py:347
  69.3 0.0 copy-start.3
  69.3 1.5 %copy.17 = bf16[128,32]{0,1:T(8,128)(2,1)} copy(bf16[128,32]{1,0:T(8,128)(2,1)} %get-tuple-element.7) | data formatting | bytes 16384 | tf_op jit(solution)/shard_map/pallas_call | solution.py:347
  70.7 1.4 %copy.18 = bf16[128,32]{0,1:T(8,128)(2,1)} copy(bf16[128,32]{1,0:T(8,128)(2,1)} %get-tuple-element.8) | data formatting | bytes 16384 | tf_op jit(solution)/shard_map/pallas_call | solution.py:347
  72.2 0.0 copy-done.3
  72.2 0.0 copy-start.2
  72.2 0.6 copy.23
  72.8 0.2 copy-done.2
  73.0 0.0 copy-start.1
  73.0 0.6 copy.24
  73.7 0.2 copy-done.1
  73.9 0.0 copy-start
  73.9 0.6 copy.25
  74.5 0.2 copy-done
  74.8 0.6 copy.26
Async XLA Ops:
  0.6 1.4 %copy-start.4 = (bf16[128,32]{0,1:T(8,128)(2,1)S(1)}, bf16[128,32]{0,1:T(8,128)(2,1)}, u32[]{:S(2)}) copy-start(bf16[128,32]{0,1:T(8,128)(2,1)} %param.10) | copy-start | bytes 24580
  69.3 2.9 %copy-start.3 = (bf16[128,256]{1,0:T(8,128)(2,1)S(1)}, bf16[128,256]{1,0:T(8,128)(2,1)}, u32[]{:S(2)}) copy-start(bf16[128,256]{1,0:T(8,128)(2,1)} %get-tuple-element.18) | copy-start | bytes 196612
  72.2 0.9 %copy-start.2 = (bf16[128,256]{1,0:T(8,128)(2,1)S(1)}, bf16[128,256]{1,0:T(8,128)(2,1)}, u32[]{:S(2)}) copy-start(bf16[128,256]{1,0:T(8,128)(2,1)} %get-tuple-element.21) | copy-start | bytes 196612
  73.0 0.9 %copy-start.1 = (bf16[128,256]{1,0:T(8,128)(2,1)S(1)}, bf16[128,256]{1,0:T(8,128)(2,1)}, u32[]{:S(2)}) copy-start(bf16[128,256]{1,0:T(8,128)(2,1)} %get-tuple-element.22) | copy-start | bytes 196612
  73.9 0.9 %copy-start = (bf16[128,256]{1,0:T(8,128)(2,1)S(1)}, bf16[128,256]{1,0:T(8,128)(2,1)}, u32[]{:S(2)}) copy-start(bf16[128,256]{1,0:T(8,128)(2,1)} %get-tuple-element.23) | copy-start | bytes 196612

commit v2 on v1

v2 whole, which is shorter than its diff:
```python
import math

import jax
import jax.numpy as jnp
import numpy as np
from jax import lax
from jax.experimental import pallas as pl
from jax.experimental.pallas import tpu as pltpu
from jax.sharding import PartitionSpec as P

HEADS = 16
KD = 16
DV = 128
WD = 128
TOK = 128
GROUP = 16
GROUPS = 4
NH = 8
ROWS = 160
SLICE = 2 * ROWS // GROUP
PER = GROUP // 2
WIDTH = HEADS * DV
EPS = 1e-06
MESH = pl.DeviceIdType.MESH
BF = jnp.bfloat16
F32 = jnp.float32


def selectors():
    first = np.zeros((2 * ROWS, 2 * KD), np.float32)
    second = np.zeros((2 * ROWS, 2 * KD), np.float32)
    for h in range(2):
        base, lane = h * ROWS, h * KD
        for i in range(KD):
            first[base + 1 + i, lane + i] = 1
            first[base + 17 + i, lane + i] = 1
            second[base + 17 + i, lane + i] = 1
        row = base + 33
        for i in range(KD):
            for j in range(i + 1, KD):
                first[row, lane + i] = 1
                second[row, lane + j] = 1
                row += 1
    return first, second


def turned(table):
    return table.reshape(2, ROWS, 2 * KD).transpose(0, 2, 1)


def nn(a, b):
    return lax.dot_general(a, b, (((1,), (0,)), ((), ())), preferred_element_type=F32)


def nt(a, b):
    return lax.dot_general(a, b, (((1,), (1,)), ((), ())), preferred_element_type=F32)


def tn(a, b):
    return lax.dot_general(a, b, (((0,), (0,)), ((), ())), preferred_element_type=F32)


def kernel(
    ql_ref, kl_ref, v_ref, wq_ref, wk_ref, gain_ref, do_ref, e1_ref, e2_ref, f1_ref, f2_ref,
    mixed_ref, gql_ref, gkl_ref, gv_ref, gwq_ref, gwk_ref,
    krim, vrim, gkout, gvout, gkin, gvin,
    st_a, r1_a, t_a, rw_a, out_a, pre_a,
    st_b, r1_b, t_b, rw_b, out_b, pre_b,
    sums, sums_in, lin_sc, win_sc, ker_sc, gvacc, gkacc, phiq_sc, phik_sc,
    ss, rs,
):
    ctx = lax.axis_index("ctx")
    head = lax.axis_index("head")
    group = ctx // GROUP
    member = lax.rem(ctx, GROUP)
    sends = []

    def partner(d):
        return lax.rem(member + d, GROUP)

    def at(g, m):
        return {"ctx": lax.rem(g, GROUPS) * GROUP + lax.rem(m, GROUP)}

    count = GROUP * GROUPS
    ahead = {"ctx": lax.rem(ctx + 1, count)}
    behind = {"ctx": lax.rem(ctx + count - 1, count)}

    barrier = pltpu.get_barrier_semaphore()
    peers = [at(group, member + d) for d in range(1, GROUP)]
    peers += [at(group + j, member) for j in (1, 2, 3)]
    peers += [ahead, behind]
    peers += [{"head": lax.rem(head + d, NH)} for d in range(1, NH)]
    for peer in peers:
        pl.semaphore_signal(barrier, inc=1, device_id=peer, device_id_type=MESH)

    def send(src, dst, slot, device):
        copy = pltpu.make_async_remote_copy(
            src_ref=src, dst_ref=dst, send_sem=ss.at[slot], recv_sem=rs.at[slot],
            device_id=device, device_id_type=MESH,
        )
        copy.start()
        sends.append(copy)
        return copy

    def wait_all(copies):
        for copy in copies:
            copy.wait_recv()

    class Scan:
        def __init__(self, sign, base, st, r1, t, rw, out, pre):
            self.sign, self.base = sign, base
            self.st, self.r1, self.t, self.rw, self.out, self.pre = st, r1, t, rw, out, pre

        def start(self):
            self.c1 = [
                send(self.st.at[partner(d)], self.r1.at[member], self.base + d - 1, at(group, member + d))
                for d in range(1, GROUP)
            ]
            self.r1[member] = self.st[member]

        def groups(self):
            wait_all(self.c1)
            total = self.r1[0].astype(F32)
            for k in range(1, GROUP):
                total = total + self.r1[k].astype(F32)
            self.t[...] = total.astype(BF)
            self.c2 = [
                send(self.t, self.rw.at[j - 1], self.base + 14 + j, at(group + j, member))
                for j in (2, 1, 3)
            ]

        def spread(self):
            wait_all(self.c2)
            total = jnp.zeros((SLICE, DV), F32)
            for j in (1, 2, 3):
                source = lax.rem(group + GROUPS - j, GROUPS)
                earlier = source < group if self.sign > 0 else source > group
                total = total + self.rw[j - 1].astype(F32) * jnp.where(earlier, 1.0, 0.0).astype(F32)
            order = range(GROUP) if self.sign > 0 else range(GROUP - 1, -1, -1)
            for k in order:
                self.out[k] = total.astype(BF)
                total = total + self.r1[k].astype(F32)
            self.c3 = [
                send(self.out.at[partner(d)], self.pre.at[member], self.base + 17 + d, at(group, member + d))
                for d in range(1, GROUP)
            ]
            self.pre[member] = self.out[member]

        def finish(self):
            wait_all(self.c3)

        def state(self, h):
            rows = [self.pre[PER * h + k].astype(F32) for k in range(PER)]
            return jnp.concatenate(rows, axis=0).astype(BF)

        def put(self, h, state):
            for k in range(PER):
                self.st[PER * h + k] = state[k * SLICE : (k + 1) * SLICE].astype(BF)

    fwd = Scan(1, 0, st_a, r1_a, t_a, rw_a, out_a, pre_a)
    bwd = Scan(-1, 33, st_b, r1_b, t_b, rw_b, out_b, pre_b)

    row32 = lax.broadcasted_iota(jnp.int32, (2 * KD, TOK), 0)
    row = lax.broadcasted_iota(jnp.int32, (TOK, TOK), 0)
    col = lax.broadcasted_iota(jnp.int32, (TOK, TOK), 1)
    causal = col <= row
    frow = lax.broadcasted_iota(jnp.int32, (ROWS, TOK), 0)
    add_first = jnp.where(frow == 0, 1.0, 0.0)
    add_second = jnp.where(frow <= KD, 1.0, 0.0)
    pair_scale = 1.0 / (math.sqrt(2.0) * math.sqrt(KD))
    scale = jnp.where(frow == 0, 1.0, jnp.where(frow <= KD, 1.0 / math.sqrt(math.sqrt(KD)), pair_scale))
    weight = jnp.where(frow >= 33, 2.0, 1.0)

    def factors(x, h):
        rows = slice(h * ROWS, (h + 1) * ROWS)
        return nn(e1_ref[rows, :], x) + add_first, nn(e2_ref[rows, :], x) + add_second

    def phi(x, h):
        a, b = factors(x, h)
        return (a * b * scale).astype(BF)

    def heavy(features):
        return (features.astype(F32) * weight).astype(BF)

    def pull(x, h, cot):
        a, b = factors(x, h)
        cot = cot * (scale * weight)
        return nn(f1_ref[h], (cot * b).astype(BF)) + nn(f2_ref[h], (cot * a).astype(BF))

    def own(x, h):
        inside = (row32 >= h * KD) & (row32 < (h + 1) * KD)
        return jnp.where(inside, x.astype(F32), 0.0).astype(BF)

    cols = [slice(h * DV, (h + 1) * DV) for h in range(2)]
    ql, kl = ql_ref[...], kl_ref[...]

    for h in range(2):
        key_phi = phi(kl, h)
        phik_sc[h] = key_phi
        fwd.put(h, nn(key_phi, v_ref[:, cols[h]]))

    pl.semaphore_wait(barrier, len(peers))
    fwd.start()

    def lin_score(h):
        return tn(own(ql, h), kl) * (1.0 / math.sqrt(KD))

    for h in range(2):
        phiq_sc[h] = phi(ql, h)
        s = lin_score(h)
        ker = jnp.where(causal, 1.0 + s + 0.5 * s * s, 0.0).astype(BF)
        ker_sc[h] = ker
        lin_sc[:, cols[h]] = nn(ker, v_ref[:, cols[h]])

    fwd.groups()
    rim = [
        send(wk_ref, krim, 66, ahead),
        send(v_ref, vrim, 67, ahead),
    ]

    scale_win = 1.0 / math.sqrt(WD)
    edge = (col > row) & (ctx > 0)
    wait_all(rim)

    def window(h):
        c = cols[h]
        q, k1, k2 = wq_ref[:, c], krim[:, c], wk_ref[:, c]
        v1, v2, do = vrim[:, c], v_ref[:, c], do_ref[:, c]
        s1 = jnp.where(edge, nt(q, k1) * scale_win, -1e30)
        s2 = jnp.where(causal, nt(q, k2) * scale_win, -1e30)
        top = jnp.maximum(
            jnp.max(s1, axis=1, keepdims=True), jnp.max(s2, axis=1, keepdims=True)
        )
        x1 = jnp.where(edge, jnp.exp(s1 - top), 0.0)
        x2 = jnp.where(causal, jnp.exp(s2 - top), 0.0)
        inv = 1.0 / (jnp.sum(x1, axis=1, keepdims=True) + jnp.sum(x2, axis=1, keepdims=True))
        p1, p2 = x1 * inv, x2 * inv
        b1, b2 = p1.astype(BF), p2.astype(BF)
        out = nn(b1, v1) + nn(b2, v2)
        win_sc[:, c] = out
        delta = jnp.sum(do.astype(F32) * out, axis=1, keepdims=True)
        g1 = (p1 * (nt(do, v1) - delta)).astype(BF)
        g2 = (p2 * (nt(do, v2) - delta)).astype(BF)
        gkout[:, c] = (tn(g1, q) * scale_win).astype(BF)
        gvout[:, c] = tn(b1, do).astype(BF)
        gwq_ref[:, c] = ((nn(g1, k1) + nn(g2, k2)) * scale_win).astype(BF)
        gkacc[:, c] = tn(g2, q) * scale_win
        gvacc[:, c] = tn(b2, do)

    window(0)
    fwd.spread()
    window(1)
    back = [
        send(gkout, gkin, 68, behind),
        send(gvout, gvin, 69, behind),
    ]
    fwd.finish()

    gain = gain_ref[...]
    for h in range(2):
        prefix = fwd.state(h)
        lin_sc[:, cols[h]] += tn(heavy(phiq_sc[h]), prefix)
    lin = lin_sc[...]
    gd = gain * do_ref[...].astype(F32)
    square = jnp.sum(lin * lin, axis=1, keepdims=True)
    cross = jnp.sum(gd * lin, axis=1, keepdims=True)
    both = jnp.where(col == 0, square, jnp.where(col == 1, cross, 0.0))
    sums[...] = both.T[:8]
    shares = [
        send(sums, sums_in.at[d - 1], 69 + d, {"head": lax.rem(head + d, NH)})
        for d in range(1, NH)
    ]
    wait_all(shares)
    total = sums[...]
    for d in range(NH - 1):
        total = total + sums_in[d]
    total = jnp.concatenate([total, jnp.zeros((TOK - 8, TOK), F32)], axis=0).T
    square = jnp.sum(jnp.where(col == 0, total, 0.0), axis=1, keepdims=True)
    cross = jnp.sum(jnp.where(col == 1, total, 0.0), axis=1, keepdims=True)
    inverse = 1.0 / jnp.sqrt(square * (1.0 / WIDTH) + EPS)
    grad_lin = (
        inverse * gd - lin * (inverse * inverse * inverse * (cross * (1.0 / WIDTH)))
    ).astype(BF)
    for h in range(2):
        bwd.put(h, nn(phiq_sc[h], grad_lin[:, cols[h]]))
    bwd.start()
    mixed_ref[...] = (lin * inverse * gain + win_sc[...]).astype(BF)

    gq = jnp.zeros((2 * KD, TOK), F32)
    gk = jnp.zeros((2 * KD, TOK), F32)
    for h in range(2):
        gl = grad_lin[:, cols[h]]
        g = nt(gl, v_ref[:, cols[h]]) * (1.0 + lin_score(h))
        g = jnp.where(causal, g, 0.0).astype(BF)
        gq = gq + nt(own(kl, h), g) * (1.0 / math.sqrt(KD))
        gk = gk + nn(own(ql, h), g) * (1.0 / math.sqrt(KD))
    bwd.groups()
    for h in range(2):
        gl = grad_lin[:, cols[h]]
        prefix = fwd.state(h)
        gq = gq + pull(ql, h, nt(prefix, gl))
        gvacc[:, cols[h]] += tn(ker_sc[h], gl)
    gql_ref[...] = gq.astype(BF)
    bwd.spread()
    wait_all(back)
    gwk_ref[...] = (gkacc[...] + gkin[...].astype(F32)).astype(BF)
    gvacc[...] += gvin[...].astype(F32)
    bwd.finish()
    for h in range(2):
        suffix = bwd.state(h)
        gv_ref[:, cols[h]] = (gvacc[:, cols[h]] + tn(heavy(phik_sc[h]), suffix)).astype(BF)
        gk = gk + pull(kl, h, nt(suffix, v_ref[:, cols[h]]))
    gkl_ref[...] = gk.astype(BF)
    for copy in sends:
        copy.wait_send()


def shards(query_lin, key_lin, values, win_queries, win_keys, gain, grad_out):
    first, second = selectors()
    wide = jax.ShapeDtypeStruct((TOK, 2 * DV), BF)
    thin = jax.ShapeDtypeStruct((2 * KD, TOK), BF)
    spec = pl.BlockSpec(memory_space=pltpu.VMEM)
    full = pltpu.VMEM((TOK, 2 * DV), BF)
    full32 = pltpu.VMEM((TOK, 2 * DV), F32)
    one = pltpu.VMEM((SLICE, DV), BF)
    three = pltpu.VMEM((GROUPS - 1, SLICE, DV), BF)
    every = pltpu.VMEM((GROUP, SLICE, DV), BF)
    scan = [every, every, one, three, every, every]
    outs = pl.pallas_call(
        kernel,
        out_shape=(wide, thin, thin, wide, wide, wide),
        in_specs=[spec] * 11,
        out_specs=(spec,) * 6,
        scratch_shapes=[full] * 6
        + scan
        + scan
        + [
            pltpu.VMEM((8, TOK), F32),
            pltpu.VMEM((NH - 1, 8, TOK), F32),
            full32,
            full32,
            pltpu.VMEM((2, TOK, TOK), BF),
            full32,
            full32,
            pltpu.VMEM((2, ROWS, TOK), BF),
            pltpu.VMEM((2, ROWS, TOK), BF),
            pltpu.SemaphoreType.DMA((77,)),
            pltpu.SemaphoreType.DMA((77,)),
        ],
        compiler_params=pltpu.CompilerParams(collective_id=0, has_side_effects=True),
    )(
        query_lin.T, key_lin.T, values, win_queries, win_keys, gain.reshape(1, -1), grad_out,
        jnp.asarray(first, BF), jnp.asarray(second, BF),
        jnp.asarray(turned(first), BF), jnp.asarray(turned(second), BF),
    )
    return outs[0], outs[1].T, outs[2].T, outs[3], outs[4], outs[5]


def solution(mesh):
    tiled = P("ctx", "head")
    return jax.shard_map(
        shards,
        mesh=mesh,
        in_specs=(tiled, tiled, tiled, tiled, tiled, P("head"), tiled),
        out_specs=(tiled,) * 6,
        check_vma=False,
    )
```

time: 75.9 us -> 64.9 us (0.86)
  the two profiles are of different devices: /device:TPU:64 before, /device:TPU:24 now
where the time goes in v2:
time: 64.9 us; the launch traced here: 64.6 us
  Pallas kernels  58.7 us (90%)
  local copies, waits for them, and re-layouts  5.17 us (8%)
  between operations  0.66 us (1%)
    pallas_call x1, Pallas kernels, shards(): pl.pallas_call(kernel, out_shape=(wide, thin, thin, wide, wide, wide), in...  58.7 us
    unnamed x16, local copies, waits for them, and re-layouts  5.17 us

profile of v2, /device:TPU:24, one launch (start us, length us, event | category | flops | bytes accessed | tf_op | source)
XLA Modules:
  0.0 64.6 jit_solution(13564234966565670232)
XLA Ops:
  0.6 58.7 %shard_map.154 = (bf16[128,256]{1,0:T(8,128)(2,1)}, bf16[32,128]{1,0:T(8,128)(2,1)}, bf16[32,128]{1,0:T(8,128)(2,1)}, bf16[128,256]{1,0:T(8,128)(2,1)}, bf16[128...) custom-call(bf16[32,128]{1,0:T(8,128)(2,1)} %bitcast.5, bf16[32,128]{1,0:T(8,128)(2,1)} %bitcast.6, bf16[128,256]{1,0:T(8,128)(2,1)} %v_ref.1, ...), custom_call_target="tpu_custom_call" | custom-call | tf_op jit(solution)/shard_map/pallas_call | solution.py:329
  59.4 0.0 copy-start.4
  59.4 0.0 copy-start.2
  59.4 1.5 %copy.23 = bf16[128,256]{1,0:T(8,128)(2,1)} copy(bf16[128,256]{1,0:T(8,128)(2,1)} %get-tuple-element.24) | data formatting | bytes 131072
  60.9 0.0 copy-done.4
  60.9 0.0 copy-start.3
  60.9 0.6 copy.24
  61.5 0.1 copy-done.3
  61.6 0.6 copy.25
  62.2 0.0 copy-done.2
  62.2 0.0 copy-start.1
  62.2 0.6 copy.26
  62.8 0.2 copy-done.1
  63.1 0.0 copy-start
  63.1 0.6 copy.27
  63.7 0.2 copy-done
  63.9 0.6 copy.28
Async XLA Ops:
  59.4 1.5 %copy-start.4 = (bf16[32,128]{1,0:T(8,128)(2,1)S(1)}, bf16[32,128]{1,0:T(8,128)(2,1)}, u32[]{:S(2)}) copy-start(bf16[32,128]{1,0:T(8,128)(2,1)} %get-tuple-element.13) | copy-start | bytes 24580
  59.4 2.8 %copy-start.2 = (bf16[128,256]{1,0:T(8,128)(2,1)S(1)}, bf16[128,256]{1,0:T(8,128)(2,1)}, u32[]{:S(2)}) copy-start(bf16[128,256]{1,0:T(8,128)(2,1)} %get-tuple-element.27) | copy-start | bytes 196612
  60.9 0.7 %copy-start.3 = (bf16[32,128]{1,0:T(8,128)(2,1)S(1)}, bf16[32,128]{1,0:T(8,128)(2,1)}, u32[]{:S(2)}) copy-start(bf16[32,128]{1,0:T(8,128)(2,1)} %get-tuple-element.14) | copy-start | bytes 24580
  62.2 0.9 %copy-start.1 = (bf16[128,256]{1,0:T(8,128)(2,1)S(1)}, bf16[128,256]{1,0:T(8,128)(2,1)}, u32[]{:S(2)}) copy-start(bf16[128,256]{1,0:T(8,128)(2,1)} %get-tuple-element.28) | copy-start | bytes 196612
  63.1 0.9 %copy-start = (bf16[128,256]{1,0:T(8,128)(2,1)S(1)}, bf16[128,256]{1,0:T(8,128)(2,1)}, u32[]{:S(2)}) copy-start(bf16[128,256]{1,0:T(8,128)(2,1)} %get-tuple-element.29) | copy-start | bytes 196612

commit v3 on v2

--- a/solution.py
+++ b/solution.py
@@ -61,13 +61,15 @@
 
 
 def kernel(
-    ql_ref, kl_ref, v_ref, wq_ref, wk_ref, gain_ref, do_ref, e1_ref, e2_ref, f1_ref, f2_ref,
+    ql_in, kl_in, v_in, wq_in, wk_in, gain_in, do_in, e1_in, e2_in, f1_in, f2_in,
     mixed_ref, gql_ref, gkl_ref, gv_ref, gwq_ref, gwk_ref,
     krim, vrim, gkout, gvout, gkin, gvin,
     st_a, r1_a, t_a, rw_a, out_a, pre_a,
     st_b, r1_b, t_b, rw_b, out_b, pre_b,
     sums, sums_in, lin_sc, win_sc, ker_sc, gvacc, gkacc, phiq_sc, phik_sc,
     ss, rs,
+    ql_ref, kl_ref, v_ref, wq_ref, wk_ref, gain_ref, do_ref, e1_ref, e2_ref, f1_ref, f2_ref,
+    local, far,
 ):
     ctx = lax.axis_index("ctx")
     head = lax.axis_index("head")
@@ -87,11 +89,22 @@
 
     barrier = pltpu.get_barrier_semaphore()
     peers = [at(group, member + d) for d in range(1, GROUP)]
-    peers += [at(group + j, member) for j in (1, 2, 3)]
+    peers += [at(group + j, member) for j in (1, 3)]
     peers += [ahead, behind]
     peers += [{"head": lax.rem(head + d, NH)} for d in range(1, NH)]
     for peer in peers:
         pl.semaphore_signal(barrier, inc=1, device_id=peer, device_id_type=MESH)
+
+    inputs = (kl_in, e1_in, e2_in, v_in, ql_in, wk_in, wq_in, do_in, gain_in, f1_in, f2_in)
+    held = (kl_ref, e1_ref, e2_ref, v_ref, ql_ref, wk_ref, wq_ref, do_ref, gain_ref, f1_ref, f2_ref)
+    fetches = [
+        pltpu.make_async_copy(source, target, local.at[i])
+        for i, (source, target) in enumerate(zip(inputs, held))
+    ]
+    for fetch in fetches:
+        fetch.start()
+    for fetch in fetches:
+        fetch.wait()
 
     def send(src, dst, slot, device):
         copy = pltpu.make_async_remote_copy(
@@ -200,6 +213,7 @@
         fwd.put(h, nn(key_phi, v_ref[:, cols[h]]))
 
     pl.semaphore_wait(barrier, len(peers))
+    pl.semaphore_signal(far, inc=1, device_id=at(group + 3, member), device_id_type=MESH)
     fwd.start()
 
     def lin_score(h):
@@ -212,6 +226,7 @@
         ker_sc[h] = ker
         lin_sc[:, cols[h]] = nn(ker, v_ref[:, cols[h]])
 
+    pl.semaphore_wait(far, 1)
     fwd.groups()
     rim = [
         send(wk_ref, krim, 66, ahead),
@@ -329,7 +344,7 @@
     outs = pl.pallas_call(
         kernel,
         out_shape=(wide, thin, thin, wide, wide, wide),
-        in_specs=[spec] * 11,
+        in_specs=[pl.BlockSpec(memory_space=pl.ANY)] * 11,
         out_specs=(spec,) * 6,
         scratch_shapes=[full] * 6
         + scan
@@ -346,6 +361,19 @@
             pltpu.VMEM((2, ROWS, TOK), BF),
             pltpu.SemaphoreType.DMA((77,)),
             pltpu.SemaphoreType.DMA((77,)),
+            pltpu.VMEM((2 * KD, TOK), BF),
+            pltpu.VMEM((2 * KD, TOK), BF),
+            full,
+            full,
+            full,
+            pltpu.VMEM((1, 2 * DV), F32),
+            full,
+            pltpu.VMEM((2 * ROWS, 2 * KD), BF),
+            pltpu.VMEM((2 * ROWS, 2 * KD), BF),
+            pltpu.VMEM((2, 2 * KD, ROWS), BF),
+            pltpu.VMEM((2, 2 * KD, ROWS), BF),
+            pltpu.SemaphoreType.DMA((11,)),
+            pltpu.SemaphoreType.REGULAR,
         ],
         compiler_params=pltpu.CompilerParams(collective_id=0, has_side_effects=True),
     )(
@@ -353,6 +381,16 @@
         jnp.asarray(first, BF), jnp.asarray(second, BF),
         jnp.asarray(turned(first), BF), jnp.asarray(turned(second), BF),
     )
+    def forward(*refs):
+        for source, target in zip(refs[:6], refs[6:]):
+            target[...] = source[...]
+
+    outs = pl.pallas_call(
+        forward,
+        out_shape=(wide, thin, thin, wide, wide, wide),
+        in_specs=[spec] * 6,
+        out_specs=(spec,) * 6,
+    )(*outs)
     return outs[0], outs[1].T, outs[2].T, outs[3], outs[4], outs[5]
 
 

time: 64.9 us -> 57.5 us (0.89)
  local copies, waits for them, and re-layouts: 5.17 us -> 0 us
  Pallas kernels: 58.7 us -> 56.5 us
    unnamed x16 -> x0, local copies, waits for them, and re-layouts: 5.17 us -> none
    pallas_call x1, Pallas kernels: 58.7 us -> 54.8 us  [shards(): pl.pallas_call(kernel, out_shape=(wide, thin, thin, wide, wide, wide), in...]
    pallas_call x0 -> x1, Pallas kernels: none -> 1.68 us  [shards(): pl.pallas_call(forward, out_shape=(wide, thin, thin, wide, wide, wide), i...]
where the time goes in v3:
time: 57.5 us; the launch traced here: 57.1 us
  Pallas kernels  56.5 us (98%)
  between operations  0.64 us (1%)
    pallas_call x1, Pallas kernels, shards(): pl.pallas_call(kernel, out_shape=(wide, thin, thin, wide, wide, wide), in...  54.8 us
    pallas_call x1, Pallas kernels, shards(): pl.pallas_call(forward, out_shape=(wide, thin, thin, wide, wide, wide), i...  1.68 us

profile of v3, /device:TPU:24, one launch (start us, length us, event | category | flops | bytes accessed | tf_op | source)
XLA Modules:
  0.0 57.1 jit_solution(10074718329257114501)
XLA Ops:
  0.6 54.8 %shard_map.154 = (bf16[128,256]{1,0:T(8,128)(2,1)}, bf16[32,128]{1,0:T(8,128)(2,1)}, bf16[32,128]{1,0:T(8,128)(2,1)}, bf16[128,256]{1,0:T(8,128)(2,1)}, bf16[128...) custom-call(bf16[32,128]{1,0:T(8,128)(2,1)} %bitcast.5, bf16[32,128]{1,0:T(8,128)(2,1)} %bitcast.6, bf16[128,256]{1,0:T(8,128)(2,1)} %v_in.1, ...), custom_call_target="tpu_custom_call" | custom-call | tf_op jit(solution)/shard_map/pallas_call | solution.py:344
  55.5 1.7 %shard_map.155 = (bf16[128,256]{1,0:T(8,128)(2,1)}, bf16[32,128]{1,0:T(8,128)(2,1)}, bf16[32,128]{1,0:T(8,128)(2,1)}, bf16[128,256]{1,0:T(8,128)(2,1)}, bf16[128...) custom-call(bf16[128,256]{1,0:T(8,128)(2,1)} %get-tuple-element.18.refs_0_, bf16[32,128]{1,0:T(8,128)(2,1)} %get-tuple-element.19.refs_1_, ...), custom_call_target="tpu_custom_call" | custom-call | tf_op jit(solution)/shard_map/pallas_call | solution.py:388

commit v4 on v3

--- a/solution.py
+++ b/solution.py
@@ -13,8 +13,10 @@
 DV = 128
 WD = 128
 TOK = 128
-GROUP = 16
-GROUPS = 4
+GROUP = 8
+GROUPS = 8
+FAR_FIRST = (4, 3, 5, 2, 6, 1, 7)
+ROUND = (2, 6, 3, 5, 1, 7, 4)
 NH = 8
 ROWS = 160
 SLICE = 2 * ROWS // GROUP
@@ -87,9 +89,13 @@
     ahead = {"ctx": lax.rem(ctx + 1, count)}
     behind = {"ctx": lax.rem(ctx + count - 1, count)}
 
+    rw_a[...] = jnp.zeros_like(rw_a)
+    rw_b[...] = jnp.zeros_like(rw_b)
+
     barrier = pltpu.get_barrier_semaphore()
-    peers = [at(group, member + d) for d in range(1, GROUP)]
-    peers += [at(group + j, member) for j in (1, 3)]
+    peers = [at(group + j, member) for j in (2, 6)]
+    peers += [at(group, member + d) for d in ROUND]
+    peers += [at(group + j, member) for j in (1, 7)]
     peers += [ahead, behind]
     peers += [{"head": lax.rem(head + d, NH)} for d in range(1, NH)]
     for peer in peers:
@@ -127,7 +133,7 @@
         def start(self):
             self.c1 = [
                 send(self.st.at[partner(d)], self.r1.at[member], self.base + d - 1, at(group, member + d))
-                for d in range(1, GROUP)
+                for d in ROUND
             ]
             self.r1[member] = self.st[member]
 
@@ -137,25 +143,32 @@
             for k in range(1, GROUP):
                 total = total + self.r1[k].astype(F32)
             self.t[...] = total.astype(BF)
-            self.c2 = [
-                send(self.t, self.rw.at[j - 1], self.base + 14 + j, at(group + j, member))
-                for j in (2, 1, 3)
-            ]
+            self.c2 = []
+            for j in FAR_FIRST:
+                copy = pltpu.make_async_remote_copy(
+                    src_ref=self.t, dst_ref=self.rw.at[j - 1],
+                    send_sem=ss.at[self.base + 6 + j], recv_sem=rs.at[self.base + 6 + j],
+                    device_id=at(group + j, member), device_id_type=MESH,
+                )
+                up = group + j < GROUPS
+                sent = up if self.sign > 0 else group + j >= GROUPS
+                got = group >= j if self.sign > 0 else group < j
+                pl.when(sent)(copy.start)
+                self.c2.append((copy, sent, got))
 
         def spread(self):
-            wait_all(self.c2)
-            total = jnp.zeros((SLICE, DV), F32)
-            for j in (1, 2, 3):
-                source = lax.rem(group + GROUPS - j, GROUPS)
-                earlier = source < group if self.sign > 0 else source > group
-                total = total + self.rw[j - 1].astype(F32) * jnp.where(earlier, 1.0, 0.0).astype(F32)
+            for copy, _, got in self.c2:
+                pl.when(got)(copy.wait_recv)
+            total = self.rw[0].astype(F32)
+            for j in range(1, GROUPS - 1):
+                total = total + self.rw[j].astype(F32)
             order = range(GROUP) if self.sign > 0 else range(GROUP - 1, -1, -1)
             for k in order:
                 self.out[k] = total.astype(BF)
                 total = total + self.r1[k].astype(F32)
             self.c3 = [
-                send(self.out.at[partner(d)], self.pre.at[member], self.base + 17 + d, at(group, member + d))
-                for d in range(1, GROUP)
+                send(self.out.at[partner(d)], self.pre.at[member], self.base + 13 + d, at(group, member + d))
+                for d in ROUND
             ]
             self.pre[member] = self.out[member]
 
@@ -171,7 +184,7 @@
                 self.st[PER * h + k] = state[k * SLICE : (k + 1) * SLICE].astype(BF)
 
     fwd = Scan(1, 0, st_a, r1_a, t_a, rw_a, out_a, pre_a)
-    bwd = Scan(-1, 33, st_b, r1_b, t_b, rw_b, out_b, pre_b)
+    bwd = Scan(-1, 21, st_b, r1_b, t_b, rw_b, out_b, pre_b)
 
     row32 = lax.broadcasted_iota(jnp.int32, (2 * KD, TOK), 0)
     row = lax.broadcasted_iota(jnp.int32, (TOK, TOK), 0)
@@ -213,7 +226,8 @@
         fwd.put(h, nn(key_phi, v_ref[:, cols[h]]))
 
     pl.semaphore_wait(barrier, len(peers))
-    pl.semaphore_signal(far, inc=1, device_id=at(group + 3, member), device_id_type=MESH)
+    for j in (2, 6):
+        pl.semaphore_signal(far, inc=1, device_id=at(group + j, member), device_id_type=MESH)
     fwd.start()
 
     def lin_score(h):
@@ -226,11 +240,11 @@
         ker_sc[h] = ker
         lin_sc[:, cols[h]] = nn(ker, v_ref[:, cols[h]])
 
-    pl.semaphore_wait(far, 1)
+    pl.semaphore_wait(far, 2)
     fwd.groups()
     rim = [
-        send(wk_ref, krim, 66, ahead),
-        send(v_ref, vrim, 67, ahead),
+        send(wk_ref, krim, 42, ahead),
+        send(v_ref, vrim, 43, ahead),
     ]
 
     scale_win = 1.0 / math.sqrt(WD)
@@ -265,10 +279,6 @@
     window(0)
     fwd.spread()
     window(1)
-    back = [
-        send(gkout, gkin, 68, behind),
-        send(gvout, gvin, 69, behind),
-    ]
     fwd.finish()
 
     gain = gain_ref[...]
@@ -282,8 +292,12 @@
     both = jnp.where(col == 0, square, jnp.where(col == 1, cross, 0.0))
     sums[...] = both.T[:8]
     shares = [
-        send(sums, sums_in.at[d - 1], 69 + d, {"head": lax.rem(head + d, NH)})
+        send(sums, sums_in.at[d - 1], 45 + d, {"head": lax.rem(head + d, NH)})
         for d in range(1, NH)
+    ]
+    back = [
+        send(gkout, gkin, 44, behind),
+        send(gvout, gvin, 45, behind),
     ]
     wait_all(shares)
     total = sums[...]
@@ -328,6 +342,8 @@
     gkl_ref[...] = gk.astype(BF)
     for copy in sends:
         copy.wait_send()
+    for copy, sent, _ in fwd.c2 + bwd.c2:
+        pl.when(sent)(copy.wait_send)
 
 
 def shards(query_lin, key_lin, values, win_queries, win_keys, gain, grad_out):
@@ -359,8 +375,8 @@
             full32,
             pltpu.VMEM((2, ROWS, TOK), BF),
             pltpu.VMEM((2, ROWS, TOK), BF),
-            pltpu.SemaphoreType.DMA((77,)),
-            pltpu.SemaphoreType.DMA((77,)),
+            pltpu.SemaphoreType.DMA((53,)),
+            pltpu.SemaphoreType.DMA((53,)),
             pltpu.VMEM((2 * KD, TOK), BF),
             pltpu.VMEM((2 * KD, TOK), BF),
             full,

time: 57.5 us -> 54.9 us (0.955)
  Pallas kernels: 56.5 us -> 54.1 us
    pallas_call x1, Pallas kernels: 54.8 us -> 52.4 us  [shards(): pl.pallas_call(kernel, out_shape=(wide, thin, thin, wide, wide, wide), in...]
where the time goes in v4:
time: 54.9 us; the launch traced here: 54.7 us
  Pallas kernels  54.1 us (99%)
  between operations  0.64 us (1%)
    pallas_call x1, Pallas kernels, shards(): pl.pallas_call(kernel, out_shape=(wide, thin, thin, wide, wide, wide), in...  52.4 us
    pallas_call x1, Pallas kernels, shards(): pl.pallas_call(forward, out_shape=(wide, thin, thin, wide, wide, wide), i...  1.68 us

profile of v4, /device:TPU:24, one launch (start us, length us, event | category | flops | bytes accessed | tf_op | source)
XLA Modules:
  0.0 54.7 jit_solution(3623040799071047931)
XLA Ops:
  0.6 52.4 %shard_map.154 = (bf16[128,256]{1,0:T(8,128)(2,1)}, bf16[32,128]{1,0:T(8,128)(2,1)}, bf16[32,128]{1,0:T(8,128)(2,1)}, bf16[128,256]{1,0:T(8,128)(2,1)}, bf16[128...) custom-call(bf16[32,128]{1,0:T(8,128)(2,1)} %bitcast.5, bf16[32,128]{1,0:T(8,128)(2,1)} %bitcast.6, bf16[128,256]{1,0:T(8,128)(2,1)} %v_in.1, ...), custom_call_target="tpu_custom_call" | custom-call | tf_op jit(solution)/shard_map/pallas_call | solution.py:360
  53.0 1.7 %shard_map.155 = (bf16[128,256]{1,0:T(8,128)(2,1)}, bf16[32,128]{1,0:T(8,128)(2,1)}, bf16[32,128]{1,0:T(8,128)(2,1)}, bf16[128,256]{1,0:T(8,128)(2,1)}, bf16[128...) custom-call(bf16[128,256]{1,0:T(8,128)(2,1)} %get-tuple-element.18.refs_0_, bf16[32,128]{1,0:T(8,128)(2,1)} %get-tuple-element.19.refs_1_, ...), custom_call_target="tpu_custom_call" | custom-call | tf_op jit(solution)/shard_map/pallas_call | solution.py:404

commit v5 on v4

--- a/solution.py
+++ b/solution.py
@@ -64,14 +64,14 @@
 
 def kernel(
     ql_in, kl_in, v_in, wq_in, wk_in, gain_in, do_in, e1_in, e2_in, f1_in, f2_in,
-    mixed_ref, gql_ref, gkl_ref, gv_ref, gwq_ref, gwk_ref,
+    mixed_out, gql_out, gkl_out, gv_out, gwq_out, gwk_out,
     krim, vrim, gkout, gvout, gkin, gvin,
     st_a, r1_a, t_a, rw_a, out_a, pre_a,
     st_b, r1_b, t_b, rw_b, out_b, pre_b,
     sums, sums_in, lin_sc, win_sc, ker_sc, gvacc, gkacc, phiq_sc, phik_sc,
     ss, rs,
     ql_ref, kl_ref, v_ref, wq_ref, wk_ref, gain_ref, do_ref, e1_ref, e2_ref, f1_ref, f2_ref,
-    local, far,
+    local, far, leave, mixed_ref, gql_ref, gkl_ref, gv_ref, gwq_ref, gwk_ref,
 ):
     ctx = lax.axis_index("ctx")
     head = lax.axis_index("head")
@@ -334,12 +334,25 @@
     wait_all(back)
     gwk_ref[...] = (gkacc[...] + gkin[...].astype(F32)).astype(BF)
     gvacc[...] += gvin[...].astype(F32)
+    leaves = [
+        pltpu.make_async_copy(source, target, leave.at[i])
+        for i, (source, target) in enumerate(
+            ((mixed_ref, mixed_out), (gql_ref, gql_out), (gwq_ref, gwq_out),
+             (gwk_ref, gwk_out), (gv_ref, gv_out), (gkl_ref, gkl_out))
+        )
+    ]
+    for copy in leaves[:4]:
+        copy.start()
     bwd.finish()
     for h in range(2):
         suffix = bwd.state(h)
         gv_ref[:, cols[h]] = (gvacc[:, cols[h]] + tn(heavy(phik_sc[h]), suffix)).astype(BF)
         gk = gk + pull(kl, h, nt(suffix, v_ref[:, cols[h]]))
+    leaves[4].start()
     gkl_ref[...] = gk.astype(BF)
+    leaves[5].start()
+    for copy in leaves:
+        copy.wait()
     for copy in sends:
         copy.wait_send()
     for copy, sent, _ in fwd.c2 + bwd.c2:
@@ -350,7 +363,6 @@
     first, second = selectors()
     wide = jax.ShapeDtypeStruct((TOK, 2 * DV), BF)
     thin = jax.ShapeDtypeStruct((2 * KD, TOK), BF)
-    spec = pl.BlockSpec(memory_space=pltpu.VMEM)
     full = pltpu.VMEM((TOK, 2 * DV), BF)
     full32 = pltpu.VMEM((TOK, 2 * DV), F32)
     one = pltpu.VMEM((SLICE, DV), BF)
@@ -361,7 +373,7 @@
         kernel,
         out_shape=(wide, thin, thin, wide, wide, wide),
         in_specs=[pl.BlockSpec(memory_space=pl.ANY)] * 11,
-        out_specs=(spec,) * 6,
+        out_specs=(pl.BlockSpec(memory_space=pl.ANY),) * 6,
         scratch_shapes=[full] * 6
         + scan
         + scan
@@ -390,6 +402,13 @@
             pltpu.VMEM((2, 2 * KD, ROWS), BF),
             pltpu.SemaphoreType.DMA((11,)),
             pltpu.SemaphoreType.REGULAR,
+            pltpu.SemaphoreType.DMA((6,)),
+            full,
+            pltpu.VMEM((2 * KD, TOK), BF),
+            pltpu.VMEM((2 * KD, TOK), BF),
+            full,
+            full,
+            full,
         ],
         compiler_params=pltpu.CompilerParams(collective_id=0, has_side_effects=True),
     )(
@@ -398,14 +417,28 @@
         jnp.asarray(turned(first), BF), jnp.asarray(turned(second), BF),
     )
     def forward(*refs):
-        for source, target in zip(refs[:6], refs[6:]):
-            target[...] = source[...]
-
+        gets = [pltpu.make_async_copy(refs[i], refs[12 + i], refs[18].at[i]) for i in range(6)]
+        puts = [pltpu.make_async_copy(refs[12 + i], refs[6 + i], refs[19].at[i]) for i in range(6)]
+        for get in gets:
+            get.start()
+        for get, put in zip(gets, puts):
+            get.wait()
+            put.start()
+        for put in puts:
+            put.wait()
+
+    slim = pltpu.VMEM((2 * KD, TOK), BF)
+    anywhere = pl.BlockSpec(memory_space=pl.ANY)
     outs = pl.pallas_call(
         forward,
         out_shape=(wide, thin, thin, wide, wide, wide),
-        in_specs=[spec] * 6,
-        out_specs=(spec,) * 6,
+        in_specs=[anywhere] * 6,
+        out_specs=(anywhere,) * 6,
+        scratch_shapes=[
+            full, slim, slim, full, full, full,
+            pltpu.SemaphoreType.DMA((6,)),
+            pltpu.SemaphoreType.DMA((6,)),
+        ],
     )(*outs)
     return outs[0], outs[1].T, outs[2].T, outs[3], outs[4], outs[5]
 

time: 54.9 us -> 54.9 us (level)
  no operation moved by 1% of the time
where the time goes in v5:
time: 54.9 us; the launch traced here: 54.7 us
  Pallas kernels  54 us (98%)
  between operations  0.64 us (1%)
    pallas_call x1, Pallas kernels, shards(): pl.pallas_call(kernel, out_shape=(wide, thin, thin, wide, wide, wide), in...  52.3 us
    pallas_call x1, Pallas kernels, shards(): pl.pallas_call(forward, out_shape=(wide, thin, thin, wide, wide, wide), i...  1.7 us

profile of v5, /device:TPU:24, one launch (start us, length us, event | category | flops | bytes accessed | tf_op | source)
XLA Modules:
  0.0 54.7 jit_solution(2061188274106406940)
XLA Ops:
  0.6 52.3 %shard_map.154 = (bf16[128,256]{1,0:T(8,128)(2,1)}, bf16[32,128]{1,0:T(8,128)(2,1)}, bf16[32,128]{1,0:T(8,128)(2,1)}, bf16[128,256]{1,0:T(8,128)(2,1)}, bf16[128...) custom-call(bf16[32,128]{1,0:T(8,128)(2,1)} %bitcast.5, bf16[32,128]{1,0:T(8,128)(2,1)} %bitcast.6, bf16[128,256]{1,0:T(8,128)(2,1)} %v_in.1, ...), custom_call_target="tpu_custom_call" | custom-call | tf_op jit(solution)/shard_map/pallas_call | solution.py:372
  53.0 1.7 %shard_map.155 = (bf16[128,256]{1,0:T(8,128)(2,1)}, bf16[32,128]{1,0:T(8,128)(2,1)}, bf16[32,128]{1,0:T(8,128)(2,1)}, bf16[128,256]{1,0:T(8,128)(2,1)}, bf16[128...) custom-call(bf16[128,256]{1,0:T(8,128)(2,1)} %get-tuple-element.18.refs_0_, bf16[32,128]{1,0:T(8,128)(2,1)} %get-tuple-element.19.refs_1_, ...), custom_call_target="tpu_custom_call" | custom-call | tf_op jit(solution)/shard_map/pallas_call | solution.py:432

commit v6 on v5

--- a/solution.py
+++ b/solution.py
@@ -229,6 +229,10 @@
     for j in (2, 6):
         pl.semaphore_signal(far, inc=1, device_id=at(group + j, member), device_id_type=MESH)
     fwd.start()
+    rim = [
+        send(wk_ref, krim, 42, ahead),
+        send(v_ref, vrim, 43, ahead),
+    ]
 
     def lin_score(h):
         return tn(own(ql, h), kl) * (1.0 / math.sqrt(KD))
@@ -242,10 +246,6 @@
 
     pl.semaphore_wait(far, 2)
     fwd.groups()
-    rim = [
-        send(wk_ref, krim, 42, ahead),
-        send(v_ref, vrim, 43, ahead),
-    ]
 
     scale_win = 1.0 / math.sqrt(WD)
     edge = (col > row) & (ctx > 0)

time: 54.9 us -> 53.5 us (0.974)
  Pallas kernels: 54 us -> 52.3 us
    pallas_call x1, Pallas kernels: 52.3 us -> 50.6 us  [shards(): pl.pallas_call(kernel, out_shape=(wide, thin, thin, wide, wide, wide), in...]
where the time goes in v6:
time: 53.5 us; the launch traced here: 52.9 us
  Pallas kernels  52.3 us (98%)
  between operations  0.64 us (1%)
    pallas_call x1, Pallas kernels, shards(): pl.pallas_call(kernel, out_shape=(wide, thin, thin, wide, wide, wide), in...  50.6 us
    pallas_call x1, Pallas kernels, shards(): pl.pallas_call(forward, out_shape=(wide, thin, thin, wide, wide, wide), i...  1.7 us

profile of v6, /device:TPU:24, one launch (start us, length us, event | category | flops | bytes accessed | tf_op | source)
XLA Modules:
  0.0 52.9 jit_solution(4431234810654797367)
XLA Ops:
  0.6 50.6 %shard_map.154 = (bf16[128,256]{1,0:T(8,128)(2,1)}, bf16[32,128]{1,0:T(8,128)(2,1)}, bf16[32,128]{1,0:T(8,128)(2,1)}, bf16[128,256]{1,0:T(8,128)(2,1)}, bf16[128...) custom-call(bf16[32,128]{1,0:T(8,128)(2,1)} %bitcast.5, bf16[32,128]{1,0:T(8,128)(2,1)} %bitcast.6, bf16[128,256]{1,0:T(8,128)(2,1)} %v_in.1, ...), custom_call_target="tpu_custom_call" | custom-call | tf_op jit(solution)/shard_map/pallas_call | solution.py:372
  51.2 1.7 %shard_map.155 = (bf16[128,256]{1,0:T(8,128)(2,1)}, bf16[32,128]{1,0:T(8,128)(2,1)}, bf16[32,128]{1,0:T(8,128)(2,1)}, bf16[128,256]{1,0:T(8,128)(2,1)}, bf16[128...) custom-call(bf16[128,256]{1,0:T(8,128)(2,1)} %get-tuple-element.18.refs_0_, bf16[32,128]{1,0:T(8,128)(2,1)} %get-tuple-element.19.refs_1_, ...), custom_call_target="tpu_custom_call" | custom-call | tf_op jit(solution)/shard_map/pallas_call | solution.py:432
